TPU v7x, 32 devices: a whole 2x2x4 slice. The times are simulated.
32 devices in a mesh: dp: 4 (over y, x), tensor: 8 (over z, core).
Axes of the slice: x: 2, y: 2, z: 4, core: 2. Of those that a mesh axis runs over, the one named last changes fastest.
Arguments:
- hidden_in: bfloat16 [8192, 2048], P(('dp', 'tensor')), parts along dimension 0, may hold values from -6 to 6
- attn_gain: float32 [2048], replicated, may hold values from 0.1 to 1.9
- attn_shift: float32 [2048], replicated, may hold values from -3 to 3
- qkv_weight: bfloat16 [2048, 6144], P(None, 'tensor'), may hold values from -4 to 4
- qkv_bias: bfloat16 [6144], P('tensor'), may hold values from -3 to 3
- out_weight: bfloat16 [2048, 2048], P('tensor'), may hold values from -0.125 to 0.125
- out_bias: float32 [2048], replicated, may hold values from -3 to 3
- mlp_gain: float32 [2048], replicated, may hold values from 0.1 to 1.9
- mlp_shift: float32 [2048], replicated, may hold values from -3 to 3
- up_weight: bfloat16 [2048, 8192], P(None, 'tensor'), may hold values from -0.125 to 0.125
- up_bias: float32 [8192], P('tensor'), may hold values from -3 to 3
- down_weight: bfloat16 [8192, 2048], P('tensor'), may hold values from -0.0625 to 0.0625
- down_bias: float32 [2048], replicated, may hold values from -3 to 3
- segment_ids: int32 [4, 2048], P('dp'), parts along dimension 0, may hold values from 0 to 7, never falling along the last dimension, each value on 1 to 1024 neighbouring positions
- prompt_lengths: int32 [4], P('dp'), parts along dimension 0, may hold values from 1024 to 2048
- page_table: int32 [512, 1], P('dp'), parts along dimension 0, may hold values from 0 to 7; in each aligned block of 128 rows (0 to 127, 128 to 255, ...) at most 32 rows name the same one
Outputs:
- layer_out: bfloat16 [8192, 2048], P(('dp', 'tensor')), parts along dimension 0
- kv_pages: bfloat16 [1024, 16, 4096], P(('dp', 'tensor')), parts along dimension 0
There are 4 independent parts, one for each index of `dp`. A program takes and returns all parts, laid end to end along the dimension named above; an argument that names none is the same for every part. Nothing has to cross between parts.
Inputs may be any that keep to these rules, and one draw needn't show every extreme that they name: `segment_ids`: along a stream document numbers never fall; a document has at most 1024 tokens. `page_table`: no device owns more than 32 pages of a part, and one owns exactly 32.
All inputs are finite; a program needn't handle non-finite values.
Results may differ from a plain program's by a relative error of at most 0.014.
Values may be sent and summed in bfloat16 or wider, within the bound.
A program may use at most 128 MiB of HBM per device.

v0:
```python
import math

import jax
import jax.numpy as jnp
from jax import lax
from jax.sharding import PartitionSpec as P

HD = 128
PAGE = 16


def partner(value, axis, apart):
    mask = 2**apart
    pairs = [(source, source ^ mask) for source in range(lax.axis_size(axis))]
    return lax.ppermute(value, axis, pairs)


def normalize(values, norm_gain, norm_shift):
    widened = values.astype(jnp.float32)
    center = jnp.mean(widened, axis=-1, keepdims=True)
    spread = jnp.mean(jnp.square(widened - center), axis=-1, keepdims=True)
    return (widened - center) * lax.rsqrt(spread + 1e-05) * norm_gain + norm_shift


def pick_rows(full_rows, quarters, streams):
    shaped = full_rows.reshape(streams, 4, -1, full_rows.shape[-1])
    return jnp.take(shaped, quarters, axis=1)


def place_rows(own_rows, peer_rows, own_quarters, peer_quarters):
    streams = own_rows.shape[0]
    quarter = own_rows.shape[2]
    columns = own_rows.shape[3]
    filled = jnp.zeros((streams, 4, quarter, columns), own_rows.dtype)
    filled = filled.at[:, own_quarters].set(own_rows).at[:, peer_quarters].set(peer_rows)
    return filled.reshape(streams * 4 * quarter, columns)


def on_device(
    hidden_in,
    attn_gain,
    attn_shift,
    qkv_weight,
    qkv_bias,
    out_weight,
    out_bias,
    mlp_gain,
    mlp_shift,
    up_weight,
    up_bias,
    down_weight,
    down_bias,
    segment_ids,
    prompt_lengths,
    page_table,
):
    devices = lax.axis_size("tensor")
    position_dev = lax.axis_index("tensor")
    parity = position_dev % 2
    lower_half = parity == 0
    tok_rows = hidden_in.shape[0]
    total_rows = tok_rows * devices
    streams = segment_ids.shape[0]
    seq_len = segment_ids.shape[1]
    quarter = seq_len // 4
    peer_weight, peer_bias, peer_out = partner((qkv_weight, qkv_bias, out_weight), "tensor", 0)
    joined_weight = jnp.concatenate(
        [
            jnp.where(lower_half, qkv_weight, peer_weight),
            jnp.where(lower_half, peer_weight, qkv_weight),
        ],
        axis=1,
    )
    joined_bias = jnp.concatenate(
        [jnp.where(lower_half, qkv_bias, peer_bias), jnp.where(lower_half, peer_bias, qkv_bias)],
        axis=0,
    ).astype(jnp.float32)
    joined_out = jnp.concatenate(
        [jnp.where(lower_half, out_weight, peer_out), jnp.where(lower_half, peer_out, out_weight)],
        axis=0,
    )
    heads_here = joined_weight.shape[1] // (3 * HD)
    layout = jnp.array([[0, 1], [2, 3]], jnp.int32)
    own_quarters = layout[parity]
    peer_quarters = layout[1 - parity]
    normed = normalize(hidden_in, attn_gain, attn_shift).astype(jnp.bfloat16)
    projected = (
        jnp.dot(
            lax.all_gather(normed, "tensor", axis=0, tiled=True),
            joined_weight,
            preferred_element_type=jnp.float32,
        )
        + joined_bias
    ).astype(jnp.bfloat16)
    own_proj = pick_rows(projected, own_quarters, streams)
    keys_vals = projected.reshape(streams, seq_len, heads_here, 3, HD)[:, :, :, 1:, :]
    own_kv = pick_rows(keys_vals.reshape(total_rows, heads_here * 2 * HD), own_quarters, streams)
    queries = own_proj.reshape(streams * 2, quarter, heads_here, 3, HD)[:, :, :, 0, :]
    block_stream = jnp.arange(streams * 2, dtype=jnp.int32) // 2
    block_quarter = jnp.tile(own_quarters, streams)
    scale_factor = 1.0 / math.sqrt(HD)

    def attend_block(inputs):
        block_queries, stream_id, quarter_id = inputs
        stream_kv = lax.dynamic_index_in_dim(keys_vals, stream_id, 0, keepdims=False)
        stream_segs = lax.dynamic_index_in_dim(segment_ids, stream_id, 0, keepdims=False)
        query_pos = quarter_id * quarter + jnp.arange(quarter, dtype=jnp.int32)
        query_seg = lax.dynamic_slice_in_dim(stream_segs, quarter_id * quarter, quarter)

        def block_scores(key_block):
            key_start = key_block * quarter
            block_kv = lax.dynamic_slice_in_dim(stream_kv, key_start, quarter, 0)
            raw_scores = (
                jnp.einsum(
                    "qhd,khd->hqk",
                    block_queries,
                    block_kv[:, :, 0, :],
                    preferred_element_type=jnp.float32,
                )
                * scale_factor
            )
            key_pos = key_start + jnp.arange(quarter, dtype=jnp.int32)
            key_seg = lax.dynamic_slice_in_dim(stream_segs, key_start, quarter)
            allowed = (key_pos[None, :] <= query_pos[:, None]) & (
                key_seg[None, :] == query_seg[:, None]
            )
            return (jnp.where(allowed[None], raw_scores, -1e30), block_kv[:, :, 1, :])

        def first_pass(key_block, state_pair):
            running_max, running_sum = state_pair
            scores = block_scores(key_block)[0]
            new_max = jnp.maximum(running_max, jnp.max(scores, axis=-1))
            running_sum = running_sum * jnp.exp(running_max - new_max) + jnp.sum(
                jnp.exp(scores - new_max[..., None]), axis=-1
            )
            return (new_max, running_sum)

        heads_block = block_queries.shape[1]
        start_state = (
            jnp.full((heads_block, quarter), -1e30, jnp.float32),
            jnp.zeros((heads_block, quarter), jnp.float32),
        )
        row_max, row_sum = lax.fori_loop(0, quarter_id + 1, first_pass, start_state)

        def second_pass(key_block, accumulated):
            scores, block_values = block_scores(key_block)
            weights = (jnp.exp(scores - row_max[..., None]) / row_sum[..., None]).astype(
                jnp.bfloat16
            )
            return accumulated + jnp.einsum(
                "hqk,khd->qhd", weights, block_values, preferred_element_type=jnp.float32
            )

        accumulated = lax.fori_loop(
            0, quarter_id + 1, second_pass, jnp.zeros((quarter, heads_block, HD), jnp.float32)
        )
        return accumulated.astype(jnp.bfloat16).reshape(quarter, heads_block * HD)

    attended = lax.map(attend_block, (queries, block_stream, block_quarter))
    attended = attended.reshape(streams, 2, quarter, heads_here * HD)
    attn_full = place_rows(attended, jnp.zeros_like(attended), own_quarters, peer_quarters)
    rows_here = attn_full
    attn_sum = lax.psum_scatter(
        jnp.dot(rows_here, joined_out, preferred_element_type=jnp.float32).astype(jnp.bfloat16),
        "tensor",
        scatter_dimension=0,
        tiled=True,
    ).astype(jnp.float32)
    residual_mid = (hidden_in.astype(jnp.float32) + attn_sum + out_bias).astype(jnp.bfloat16)
    normed_mid = normalize(residual_mid, mlp_gain, mlp_shift).astype(jnp.bfloat16)
    lifted = (
        jnp.dot(
            lax.all_gather(normed_mid, "tensor", axis=0, tiled=True),
            up_weight,
            preferred_element_type=jnp.float32,
        )
        + up_bias
    )
    expanded = jax.nn.gelu(lifted, approximate=False).astype(jnp.bfloat16)
    rows_here = expanded
    mlp_sum = lax.psum_scatter(
        jnp.dot(rows_here, down_weight, preferred_element_type=jnp.float32).astype(jnp.bfloat16),
        "tensor",
        scatter_dimension=0,
        tiled=True,
    ).astype(jnp.float32)
    layer_out = (residual_mid.astype(jnp.float32) + mlp_sum + down_bias).astype(jnp.bfloat16)
    blocks_total = streams * seq_len // PAGE
    capacity = 2 * blocks_total // devices
    owners = page_table[:, 0]
    onehot = (owners[:, None] == jnp.arange(devices, dtype=jnp.int32)[None, :]).astype(jnp.int32)
    earlier = jnp.cumsum(onehot, axis=0) - onehot
    slot_ids = owners * capacity + jnp.sum(earlier * onehot, axis=1)
    per_quarter = quarter // PAGE
    own_blocks = (
        jnp.arange(streams, dtype=jnp.int32)[:, None, None] * (seq_len // PAGE)
        + own_quarters[None, :, None] * per_quarter
        + jnp.arange(per_quarter, dtype=jnp.int32)[None, None, :]
    ).reshape(-1)
    own_slots = jnp.take(slot_ids, own_blocks)
    own_pos = (
        own_quarters[None, :, None] * quarter + jnp.arange(quarter, dtype=jnp.int32)[None, None, :]
    )
    live_mask = (own_pos < prompt_lengths[:, None, None]).astype(jnp.bfloat16)
    kept_rows = own_kv * live_mask[..., None]
    page_cols = kept_rows.shape[-1]
    outgoing = (
        jnp.zeros((devices * capacity, PAGE, page_cols), jnp.bfloat16)
        .at[own_slots]
        .set(kept_rows.reshape(-1, PAGE, page_cols))
    )
    incoming = lax.all_to_all(
        outgoing.reshape(devices, capacity, PAGE, page_cols),
        "tensor",
        split_axis=0,
        concat_axis=0,
        tiled=True,
    )
    paired = incoming.reshape(devices // 2, 2, capacity, PAGE, page_cols)
    combined = paired[:, 0] + paired[:, 1]
    kv_pages = combined.transpose(1, 2, 0, 3).reshape(capacity, PAGE, devices // 2 * page_cols)
    return (layer_out, kv_pages)


def solution(mesh):
    in_specs = (
        P(("dp", "tensor"), None),
        P(),
        P(),
        P(None, "tensor"),
        P("tensor"),
        P("tensor", None),
        P(),
        P(),
        P(),
        P(None, "tensor"),
        P("tensor"),
        P("tensor", None),
        P(),
        P("dp", None),
        P("dp"),
        P("dp", None),
    )
    out_specs = (P(("dp", "tensor"), None), P(("dp", "tensor"), None, None))
    return jax.shard_map(
        on_device, mesh=mesh, in_specs=in_specs, out_specs=out_specs, check_vma=False
    )
```

profile of v0, /device:TPU:0, one launch (start us, length us, event | category | flops | bytes accessed | tf_op | source)
XLA Modules:
  0.0 703.7 jit_solution(1213690228143826244)
XLA Ops:
  7.2 1.6 convert_reduce_fusion.1
  8.8 1.6 fusion.74
  10.5 2.7 fusion.77
  13.3 0.5 collective-permute-start
  13.9 0.4 collective-permute-start.1
  14.3 0.5 fusion.90
  14.9 4.1 collective-permute-done.1
  19.0 1.8 collective-permute-done.2
  20.8 3.0 broadcast_select_fusion.3
  23.8 5.3 broadcast_select_fusion.1
  29.2 69.0 %all-gather.3.cloned.1.call-done = bf16[2048,2048]{1,0:T(8,128)(2,1)} async-done(((bf16[256,2048]{1,0:T(8,128)(2,1)}), bf16[2048,2048]{1,0:T(8,128)(2,1)}) %all-gather.3.cloned.1.call-update) | async-done | bytes 8388624 | tf_op jit(solution)/shard_map/all_gather | solution.py:89
  98.1 18.6 %add_convert_fusion = bf16[2048,1536]{1,0:T(8,128)(2,1)} fusion(bf16[2048,2048]{1,0:T(8,128)(2,1)} %all-gather.3.cloned.1.call-done, bf16[2048,768]{1,0:T(8,128)(2,1)} %get-tuple-element.288, bf16[2048,768]{1,0:T(8,128)(2,1)} %get-tuple-element.287, f32[1536]{0:T(1024)S(1)} %maximum_convert_fusion), kind=kOutput, calls=%fused_computation.38 | convolution fusion | flops 12903776256 | bytes 20977664 | tf_op jit(solution)/shard_map/dot_general | solution.py:88
  116.7 8.6 %copy.32 = bf16[2048,1536]{0,1:T(8,128)(2,1)} copy(bf16[2048,1536]{1,0:T(8,128)(2,1)} %add_convert_fusion) | data formatting | bytes 12582912 | tf_op jit(solution)/shard_map/convert_element_type | solution.py:94
  125.4 4.8 slice.34
  130.1 6.2 copy.34
  136.4 3.5 gather_fusion
  139.9 2.8 copy.33
  142.8 1.4 fusion.85
  144.2 1.0 broadcast_in_dim.101.clone2
  145.2 27.5 %while.44 = (s32[]{:T(128)}, bf16[2,512,512]{2,1,0:T(8,128)(2,1)}, s32[2]{0:T(128)S(1)}, bf16[1,2048,4,2,128]{4,1,2,3,0:T(8,128)(2,1)}, bf16[2,512,4,128]{1,3,2,...) while((s32[]{:T(128)}, bf16[2,512,512]{2,1,0:T(8,128)(2,1)}, ...), condition=%wide.region_9.10_spmd, body=%wide.region_2.0_spmd.sunk | while | flops 819992576 | bytes 21412772 | solution.py:159
  145.2 0.7 dynamic_slice.65
  147.6 3.3 while.45
  147.7 0.3 compare_and_fusion.5
  148.0 1.9 fusion.139
  150.0 0.9 exponential_reduce_fusion.2
  151.0 3.4 while.46
  151.2 0.3 compare_and_fusion.6
  151.4 3.0 fusion.141
  154.8 0.8 constant_dynamic-update-slice_fusion.2
  155.6 0.7 dynamic_slice.65
  158.0 6.6 while.45
  158.1 0.3 compare_and_fusion.5
  158.4 1.9 fusion.139
  160.3 0.9 exponential_reduce_fusion.2
  161.4 0.3 compare_and_fusion.5
  161.7 1.9 fusion.139
  163.6 0.9 exponential_reduce_fusion.2
  164.7 6.8 while.46
  164.8 0.3 compare_and_fusion.6
  165.1 3.0 fusion.141
  168.2 0.3 compare_and_fusion.6
  168.5 3.0 fusion.141
  171.8 0.8 constant_dynamic-update-slice_fusion.2
  172.8 1.9 scatter_fusion
  174.9 0.8 scatter_fusion.1
  175.6 8.2 %convolution_convert_fusion.1 = bf16[2048,2048]{1,0:T(8,128)(2,1)} fusion(bf16[2048,512]{1,0:T(8,128)(2,1)S(1)} %bitcast.147, bf16[256,2048]{1,0:T(8,128)(2,1)} %get-tuple-element.290, bf16[256,2048]{1,0:T(8,128)(2,1)} %get-tuple-element.289), kind=kOutput, calls=%fused_computation.58 | convolution fusion | flops 4303355904 | bytes 12582912 | tf_op jit(solution)/shard_map/dot_general | solution.py:164
  184.0 114.8 %reduce-scatter.3.cloned.1.call-done = bf16[256,2048]{1,0:T(8,128)(2,1)} async-done(((bf16[2048,2048]{1,0:T(8,128)(2,1)}), bf16[256,2048]{1,0:T(8,128)(2,1)}) %reduce-scatter.3.cloned.1.call-update) | async-done | bytes 1048592 | tf_op jit(solution)/shard_map/reduce_scatter | solution.py:163
  298.8 1.8 convert_reduce_fusion
  300.6 0.4 fusion.70
  301.1 1.4 fusion.73
  302.6 80.5 %all-gather.5.cloned.1.call-done = bf16[2048,2048]{1,0:T(8,128)(2,1)} async-done(((bf16[256,2048]{1,0:T(8,128)(2,1)}), bf16[2048,2048]{1,0:T(8,128)(2,1)}) %all-gather.5.cloned.1.call-update) | async-done | bytes 8388624 | tf_op jit(solution)/shard_map/all_gather | solution.py:173
  383.1 41.8 %convolution_convert_fusion = bf16[2048,2048]{1,0:T(8,128)(2,1)} fusion(bf16[1024,2048]{1,0:T(8,128)(2,1)} %param.34, bf16[2048,2048]{1,0:T(8,128)(2,1)} %all-gather.5.cloned.1.call-done, bf16[2048,1024]{1,0:T(8,128)(2,1)} %param.32, f32[1024]{0:T(1024)S(1)} %copy-done.17), kind=kOutput, calls=%fused_computation.57 | convolution fusion | flops 17322475520 | bytes 25169920 | tf_op jit(solution)/shard_map/dot_general | solution.py:182
  425.0 0.6 copy-done.11
  427.3 0.8 gather_fusion.1
  428.2 7.9 %reshape.484 = bf16[4,512,1024]{1,0,2:T(4,128)(2,1)} reshape(bf16[1,2048,4,2,128]{1,4,3,2,0:T(8,128)(2,1)} %slice.34) | data formatting | bytes 8388608 | tf_op jit(solution)/shard_map/reshape;reshape | solution.py:26
  436.1 7.5 %copy.42 = bf16[4,512,1024]{2,1,0:T(8,128)(2,1)} copy(bf16[4,512,1024]{1,0,2:T(4,128)(2,1)} %reshape.484) | data formatting | bytes 8388608 | tf_op jit(solution)/shard_map/reshape;reshape | solution.py:26
  443.6 4.3 gather_fusion.2
  447.9 1.9 select_multiply_fusion
  449.9 4.3 broadcast_in_dim.105
  454.2 8.6 %scatter_fusion.2 = bf16[256,16,1024]{2,1,0:T(8,128)(2,1)} fusion(bf16[256,16,1024]{2,1,0:T(8,128)(2,1)} %broadcast_in_dim.105, s32[64]{0:T(128)S(1)} %fusion.91, bf16[64,16,1024]{2,1,0:T(8,128)(2,1)S(1)} %select_multiply_fusion), kind=kCustom, calls=%fused_computation.5 | custom fusion | bytes 6291712 | tf_op jit(solution)/shard_map/scatter | solution.py:210
  462.8 228.6 %all_to_all.5 = bf16[8,32,16,1024]{3,2,1,0:T(8,128)(2,1)S(1)} all-to-all(bf16[8,32,16,1024]{3,2,1,0:T(8,128)(2,1)} %bitcast.143), channel_id=1, replica_groups=mesh['dp'=4,'tensor'=8] {'tensor'}, dimensions={0} | all-to-all | bytes 16777216 | tf_op jit(solution)/shard_map/all_to_all | solution.py:212
  691.4 0.4 fusion.34
  691.9 2.7 copy.46
  694.6 2.6 fusion.81
  (112 shorter events, 3.8 us)
Async XLA Ops:
  7.2 7.1 %copy-start.10 = (s32[2,2]{1,0:T(2,128)S(1)}, s32[2,2]{1,0:T(2,128)}, u32[]{:S(2)}) copy-start(s32[2,2]{1,0:T(2,128)} %constant.233.clone) | copy-start | bytes 52
  7.2 6.1 copy-start.1
  7.2 6.7 copy-start.13
  7.2 90.9 %all-gather.3.cloned.1.call-start = ((), (), s32[]{:S(2)}) async-start(), calls=%async_computation.3 | async-start | bytes 9437184 | tf_op jit(solution)/shard_map/all_gather | solution.py:89
  13.2 285.6 %reduce-scatter.3.cloned.1.call-start = ((), (), s32[]{:S(2)}) async-start(), calls=%async_computation.4 | async-start | bytes 9437184 | tf_op jit(solution)/shard_map/reduce_scatter | solution.py:163
  13.3 10.6 %collective-permute-start = (bf16[2048,768]{1,0:T(8,128)(2,1)S(1)}, bf16[2048,768]{1,0:T(8,128)(2,1)}, u32[]{:S(2)}, u32[]{:S(2)}) collective-permute-start(bf16[2048,768]{1,0:T(8,128)(2,1)S(1)} %copy-done.1), channel_id=1, source_target_pairs={{0,1},{1,0},{2,3},{3,2},{4,5},{5,4},{6,7},{7,6},{8,9},{9,8},{10,11... | collective-permute-start | bytes 9437192 | tf_op jit(solution)/shard_map/ppermute | solution.py:15
  13.8 7.1 %collective-permute-start.2 = (bf16[256,2048]{1,0:T(8,128)(2,1)}, bf16[256,2048]{1,0:T(8,128)(2,1)}, u32[]{:S(2)}, u32[]{:S(2)}) collective-permute-start(bf16[256,2048]{1,0:T(8,128)(2,1)} %param.28), channel_id=1, source_target_pairs={{0,1},{1,0},{2,3},{3,2},{4,5},{5,4},{6,7},{7,6},{8,9},{9,8},{10,11... | collective-permute-start | bytes 3145736 | tf_op jit(solution)/shard_map/ppermute | solution.py:15
  13.9 5.1 collective-permute-start.1
  14.3 128.5 %copy-start.15 = (pred[2]{0:T(512)(128)(4,1)}, pred[2]{0:T(512)(128)(4,1)S(1)}, u32[]{:S(2)}) copy-start(pred[2]{0:T(512)(128)(4,1)S(1)} %compare_and_fusion.2) | copy-start | bytes 10
  14.9 4.1 copy-start.8
  14.9 121.5 %copy-start.7 = (s32[1024]{0:T(1024)}, s32[1024]{0:T(1024)S(1)}, u32[]{:S(2)}) copy-start(s32[1024]{0:T(1024)S(1)} %pad_clamp_fusion.1) | copy-start | bytes 12292
  139.9 5.3 copy-start.2
  145.2 27.6 %copy-start.9 = (s32[2]{0:T(128)S(1)}, s32[2]{0:T(128)}, u32[]{:S(2)}) copy-start(s32[2]{0:T(128)} %copy-done.8) | copy-start | bytes 28
  172.7 2.2 copy-start.14
  183.9 115.0 %copy-start = (bf16[256,2048]{1,0:T(8,128)(2,1)S(1)}, bf16[256,2048]{1,0:T(8,128)(2,1)}, u32[]{:S(2)}) copy-start(bf16[256,2048]{1,0:T(8,128)(2,1)} %param.23) | copy-start | bytes 3145732
  183.9 115.0 %copy-start.3 = (f32[2048]{0:T(1024)S(1)}, f32[2048]{0:T(1024)}, u32[]{:S(2)}) copy-start(f32[2048]{0:T(1024)} %param.29) | copy-start | bytes 24580
  183.9 117.2 %copy-start.4 = (f32[2048]{0:T(1024)S(1)}, f32[2048]{0:T(1024)}, u32[]{:S(2)}) copy-start(f32[2048]{0:T(1024)} %param.31) | copy-start | bytes 24580
  183.9 117.2 %copy-start.5 = (f32[2048]{0:T(1024)S(1)}, f32[2048]{0:T(1024)}, u32[]{:S(2)}) copy-start(f32[2048]{0:T(1024)} %param.30) | copy-start | bytes 24580
  183.9 199.2 %copy-start.17 = (f32[1024]{0:T(1024)S(1)}, f32[1024]{0:T(1024)}, u32[]{:S(2)}) copy-start(f32[1024]{0:T(1024)} %param.33) | copy-start | bytes 12292
  183.9 199.2 %all-gather.5.cloned.1.call-start = ((), (), s32[]{:S(2)}) async-start(), calls=%async_computation.5 | async-start | bytes 9437184 | tf_op jit(solution)/shard_map/all_gather | solution.py:173
  302.5 392.0 %reduce-scatter.5.cloned.1.call-start = ((), (), s32[]{:S(2)}) async-start(), calls=%async_computation.6 | async-start | bytes 9437184 | tf_op jit(solution)/shard_map/reduce_scatter | solution.py:181
  425.0 0.7 copy-start.11
  425.0 1.5 copy-start.16
  425.0 1.9 copy-start.12
  691.9 2.7 copy-start.6
Sparse Core Ops, SparseCore 0:
  13.3 84.7 all-gather.2
  184.0 114.7 reduce-scatter.2
  302.7 80.4 all-gather.4
  425.1 140.0 reduce-scatter.4
where the time goes:
time: 706 us; the launch traced here: 704 us
  waiting for transfers between devices  270 us (38%)
  blocking collectives  229 us (32%)
  matrix products  83.5 us (12%)
  local copies, waits for them, and re-layouts  72.2 us (10%)
  other arithmetic  30 us (4%)
  between operations  14.7 us (2%)
    all_to_all x1, blocking collectives, on_device(): lax.all_to_all(outgoing.reshape(devices, capacity, PAGE, page_cols), 'ten...  229 us
    reduce_scatter x1, waiting for transfers between devices, on_device(): lax.psum_scatter(jnp.dot(rows_here, joined_out, preferred_element_type=jn...  115 us
    all_gather x1, waiting for transfers between devices, on_device(): lax.all_gather(normed_mid, 'tensor', axis=0, tiled=True)  80.5 us
    all_gather x1, waiting for transfers between devices, on_device(): lax.all_gather(normed, 'tensor', axis=0, tiled=True)  69 us
    dot_general x1, matrix products, on_device(): jnp.dot(rows_here, down_weight, preferred_element_type=jnp.float32)  41.8 us
    dot_general x1, matrix products, on_device(): jnp.dot(lax.all_gather(normed, 'tensor', axis=0, tiled=True), joined_weig...  18.6 us
    another operation x2, local copies, waits for them, and re-layouts, pick_rows(): shaped = full_rows.reshape(streams, 4, -1, full_rows.shape[-1])  15.3 us
  transfers between devices with their start and end apart: 7, of which 5 were waited for; matrix products, arithmetic and copies ran while one was open for 7% of the time, Pallas kernels for 0%

commit v1 on v0

v1 whole, which is shorter than its diff:
```python
import functools
import math

import jax
import jax.numpy as jnp
from jax import lax
from jax.experimental import pallas as pl
from jax.experimental.pallas import tpu as pltpu
from jax.sharding import PartitionSpec as P

HD = 128
PAGE = 16
MAX_DOC = 1024
Q_BLOCK = 256
CHUNKS = 2


def normalize(values, norm_gain, norm_shift):
    widened = values.astype(jnp.float32)
    center = jnp.mean(widened, axis=-1, keepdims=True)
    spread = jnp.mean(jnp.square(widened - center), axis=-1, keepdims=True)
    return (widened - center) * lax.rsqrt(spread + 1e-05) * norm_gain + norm_shift


def attend_kernel(window, seq_len, q_ref, k_ref, v_ref, qseg_ref, kseg_ref, out_ref):
    block = pl.program_id(2)
    rows = q_ref.shape[0]
    start = jnp.clip(block * rows - MAX_DOC, 0, seq_len - window)
    start = pl.multiple_of(start, 128)
    keys = k_ref[pl.ds(start, window), :]
    values = v_ref[pl.ds(start, window), :]
    scores = lax.dot_general(
        q_ref[...], keys, (((1,), (1,)), ((), ())), preferred_element_type=jnp.float32
    ) * (1.0 / math.sqrt(HD))
    query_pos = block * rows + lax.broadcasted_iota(jnp.int32, (rows, window), 0)
    key_pos = start + lax.broadcasted_iota(jnp.int32, (rows, window), 1)
    allowed = (key_pos <= query_pos) & (qseg_ref[...] == kseg_ref[0, :, pl.ds(start, window)])
    scores = jnp.where(allowed, scores, -1e30)
    expo = jnp.exp(scores - jnp.max(scores, axis=1, keepdims=True))
    weights = (expo * (1.0 / jnp.sum(expo, axis=1, keepdims=True))).astype(jnp.bfloat16)
    out_ref[...] = jnp.dot(weights, values, preferred_element_type=jnp.float32).astype(
        jnp.bfloat16
    )


def attend(projected, segment_ids):
    streams, seq_len = segment_ids.shape
    heads = projected.shape[1] // (3 * HD)
    blocks = seq_len // Q_BLOCK
    window = min(seq_len, MAX_DOC + Q_BLOCK)
    pairs = streams * heads * seq_len * window
    return pl.pallas_call(
        functools.partial(attend_kernel, window, seq_len),
        grid=(streams, heads, blocks),
        in_specs=[
            pl.BlockSpec((Q_BLOCK, HD), lambda s, n, i: (s * blocks + i, 3 * n)),
            pl.BlockSpec((seq_len, HD), lambda s, n, i: (s, 3 * n + 1)),
            pl.BlockSpec((seq_len, HD), lambda s, n, i: (s, 3 * n + 2)),
            pl.BlockSpec((Q_BLOCK, 1), lambda s, n, i: (s * blocks + i, 0)),
            pl.BlockSpec((1, 1, seq_len), lambda s, n, i: (s, 0, 0)),
        ],
        out_specs=pl.BlockSpec((Q_BLOCK, HD), lambda s, n, i: (s * blocks + i, n)),
        out_shape=jax.ShapeDtypeStruct((streams * seq_len, heads * HD), jnp.bfloat16),
        compiler_params=pltpu.CompilerParams(vmem_limit_bytes=24 << 20),
        cost_estimate=pl.CostEstimate(
            flops=4 * pairs * HD,
            bytes_accessed=2 * projected.size * 2,
            transcendentals=pairs,
        ),
    )(
        projected,
        projected,
        projected,
        segment_ids.reshape(streams * seq_len, 1),
        segment_ids.reshape(streams, 1, seq_len),
    )


def join_pair(value, axis, position):
    devices = lax.axis_size("tensor")
    other = lax.ppermute(value, "tensor", [(source, source ^ 1) for source in range(devices)])
    first = jnp.where(position % 2 == 0, value, other)
    second = jnp.where(position % 2 == 0, other, value)
    return jnp.concatenate([first, second], axis=axis)


def pack_pages(page_rows, page_table, capacity, position):
    devices = lax.axis_size("tensor")
    pages = page_rows.shape[0]
    owners = page_table[:, 0]
    onehot = (owners[:, None] == jnp.arange(devices, dtype=jnp.int32)[None, :]).astype(jnp.int32)
    ranks = jnp.sum((jnp.cumsum(onehot, axis=0) - onehot) * onehot, axis=1)
    slot_ids = owners * capacity + ranks
    hits = slot_ids[None, :] == jnp.arange(devices * capacity, dtype=jnp.int32)[:, None]
    taken = jnp.any(hits, axis=1)
    source_page = jnp.sum(
        jnp.where(hits, jnp.arange(pages, dtype=jnp.int32)[None, :], 0), axis=1
    )
    outgoing = jnp.where(
        taken[:, None, None], jnp.take(page_rows, source_page, axis=0, mode="clip"), 0
    ).astype(jnp.bfloat16)
    outgoing = outgoing.reshape((devices, capacity) + page_rows.shape[1:])
    return [
        lax.dynamic_index_in_dim(outgoing, position ^ apart, 0, keepdims=False)
        for apart in range(devices)
    ]


def send_pages(pieces):
    devices = len(pieces)
    received = [pieces[0]]
    for apart in range(1, devices):
        hops = [(source, source ^ apart) for source in range(devices)]
        received.append(lax.ppermute(pieces[apart], "tensor", hops))
    return received


def lay_out_pages(received, position):
    devices = len(received)
    stacked = jnp.stack(received)
    origins = position ^ jnp.arange(devices, dtype=jnp.int32)
    ordered = jnp.take(stacked, origins, axis=0, mode="clip")
    return ordered.transpose(1, 2, 0, 3).reshape(ordered.shape[1], ordered.shape[2], -1)


def on_device(
    hidden_in,
    attn_gain,
    attn_shift,
    qkv_weight,
    qkv_bias,
    out_weight,
    out_bias,
    mlp_gain,
    mlp_shift,
    up_weight,
    up_bias,
    down_weight,
    down_bias,
    segment_ids,
    prompt_lengths,
    page_table,
):
    devices = lax.axis_size("tensor")
    position = lax.axis_index("tensor")
    tok_rows, width = hidden_in.shape
    total_rows = tok_rows * devices
    streams, seq_len = segment_ids.shape
    whole_heads = qkv_weight.shape[1] % (3 * HD) == 0

    normed = normalize(hidden_in, attn_gain, attn_shift).astype(jnp.bfloat16)
    if not whole_heads:
        qkv_weight = join_pair(qkv_weight, 1, position)
        qkv_bias = join_pair(qkv_bias, 0, position)
    gathered = lax.all_gather(normed, "tensor", axis=0, tiled=True)
    projected = (
        jnp.dot(gathered, qkv_weight, preferred_element_type=jnp.float32)
        + qkv_bias.astype(jnp.float32)
    ).astype(jnp.bfloat16)
    heads_here = projected.shape[1] // (3 * HD)
    attended = attend(projected, segment_ids)
    keys_vals = projected.reshape(total_rows, heads_here, 3 * HD)[:, :, HD:]
    keys_vals = keys_vals.reshape(total_rows, heads_here * 2 * HD)
    if not whole_heads:
        half = attended.shape[1] // 2
        attended = lax.dynamic_slice_in_dim(attended, position % 2 * half, half, 1)
        half = keys_vals.shape[1] // 2
        keys_vals = lax.dynamic_slice_in_dim(keys_vals, position % 2 * half, half, 1)

    blocks_total = total_rows // PAGE
    live = jnp.arange(seq_len, dtype=jnp.int32)[None, :] < prompt_lengths[:, None]
    kept_rows = jnp.where(live.reshape(total_rows, 1), keys_vals, 0).astype(jnp.bfloat16)
    pieces = pack_pages(
        kept_rows.reshape(blocks_total, PAGE, -1),
        page_table,
        2 * blocks_total // devices,
        position,
    )
    attended, pieces = lax.optimization_barrier((attended, pieces))
    received = send_pages(pieces)

    part = tok_rows // CHUNKS
    shaped = attended.reshape(devices, CHUNKS, part, attended.shape[1])
    sums = []
    for chunk in range(CHUNKS):
        rows = shaped[:, chunk].reshape(devices * part, -1)
        terms = jnp.dot(rows, out_weight, preferred_element_type=jnp.float32)
        sums.append(
            lax.psum_scatter(
                terms.astype(jnp.bfloat16), "tensor", scatter_dimension=0, tiled=True
            )
        )
    residuals, gathers = [], []
    for chunk in range(CHUNKS):
        hidden = lax.slice_in_dim(hidden_in, chunk * part, (chunk + 1) * part, axis=0)
        attn_sum = sums[chunk]
        if chunk > 0:
            attn_sum, residuals[-1], _ = lax.optimization_barrier(
                (attn_sum, residuals[-1], normed_mid)
            )
        residual_mid = (
            hidden.astype(jnp.float32) + attn_sum.astype(jnp.float32) + out_bias
        ).astype(jnp.bfloat16)
        normed_mid = normalize(residual_mid, mlp_gain, mlp_shift).astype(jnp.bfloat16)
        residuals.append(residual_mid)
        gathers.append(lax.all_gather(normed_mid, "tensor", axis=0, tiled=True))
    sums = []
    for chunk in range(CHUNKS):
        lifted = jnp.dot(gathers[chunk], up_weight, preferred_element_type=jnp.float32) + up_bias
        expanded = jax.nn.gelu(lifted, approximate=False).astype(jnp.bfloat16)
        if chunk == 0:
            expanded, received = lax.optimization_barrier((expanded, received))
        else:
            expanded = lax.optimization_barrier(expanded)
        terms = jnp.dot(expanded, down_weight, preferred_element_type=jnp.float32)
        sums.append(
            lax.psum_scatter(
                terms.astype(jnp.bfloat16), "tensor", scatter_dimension=0, tiled=True
            )
        )
    kv_pages = lay_out_pages(received, position)
    outs = [
        (residual_mid.astype(jnp.float32) + mlp_sum.astype(jnp.float32) + down_bias).astype(
            jnp.bfloat16
        )
        for residual_mid, mlp_sum in zip(residuals, sums)
    ]
    layer_out = outs[0] if CHUNKS == 1 else jnp.concatenate(outs, axis=0)
    return (layer_out, kv_pages)


def solution(mesh):
    in_specs = (
        P(("dp", "tensor"), None),
        P(),
        P(),
        P(None, "tensor"),
        P("tensor"),
        P("tensor", None),
        P(),
        P(),
        P(),
        P(None, "tensor"),
        P("tensor"),
        P("tensor", None),
        P(),
        P("dp", None),
        P("dp"),
        P("dp", None),
    )
    out_specs = (P(("dp", "tensor"), None), P(("dp", "tensor"), None, None))
    return jax.shard_map(
        on_device, mesh=mesh, in_specs=in_specs, out_specs=out_specs, check_vma=False
    )
```

time: 706 us -> 535 us (0.76)
  blocking collectives: 229 us -> 0 us
  waiting for transfers between devices: 270 us -> 369 us
  local copies, waits for them, and re-layouts: 72.2 us -> 46.3 us
  matrix products: 83.5 us -> 61.3 us
  Pallas kernels: 0 us -> 18.6 us
  other arithmetic: 30 us -> 18.1 us
    all_to_all x1 -> x0, blocking collectives: 229 us -> none  [on_device(): lax.all_to_all(outgoing.reshape(devices, capacity, PAGE, page_cols), 'ten...]
    ppermute x3 -> x7, waiting for transfers between devices: 5.91 us -> 47.9 us  [send_pages(): received.append(lax.ppermute(pieces[apart], 'tensor', hops))]
    reduce_scatter x2 -> x4, waiting for transfers between devices: 115 us -> 150 us  [on_device(): lax.psum_scatter(terms.astype(jnp.bfloat16), 'tensor', scatter_dimension=...]
    dot_general x9 -> x7, matrix products: 83.5 us -> 61.3 us  [the longest x2 32.5 us: on_device(): jnp.dot(gathers[chunk], up_weight, preferred_element_type=jnp.float32)]
    all_gather x2 -> x3, waiting for transfers between devices: 149 us -> 170 us  [the longest x2 88.4 us: on_device(): gathers.append(lax.all_gather(normed_mid, 'tensor', axis=0, tiled=True))]
    pallas_call x0 -> x1, Pallas kernels: none -> 18.6 us  [attend(): pl.pallas_call(functools.partial(attend_kernel, window, seq_len), grid=(s...]
    reshape x1 -> x4, local copies, waits for them, and re-layouts: 2.68 us -> 17.9 us  [the longest x1 7.02 us: on_device(): keys_vals = projected.reshape(total_rows, heads_here, 3 * HD)[:, :, HD:]]
    another operation x8 -> x1, local copies, waits for them, and re-layouts: 15.6 us -> 1.88 us  [lay_out_pages(): stacked = jnp.stack(received)]
  transfers between devices with their start and end apart: 7 -> 14, of which waited for: 5 -> 8; matrix products, arithmetic and copies ran while one was open for 7% -> 14% of each run, Pallas kernels for 0% -> 0%
where the time goes in v1:
time: 535 us
  waiting for transfers between devices  369 us (69%)
  matrix products  61.3 us (11%)
  local copies, waits for them, and re-layouts  46.3 us (9%)
  Pallas kernels  18.6 us (3%)
  other arithmetic  18.1 us (3%)
  between operations  15.2 us (3%)
  starting transfers between devices  6.46 us (1%)
    reduce_scatter x4, waiting for transfers between devices, on_device(): lax.psum_scatter(terms.astype(jnp.bfloat16), 'tensor', scatter_dimension=...  150 us
    all_gather x2, waiting for transfers between devices, on_device(): gathers.append(lax.all_gather(normed_mid, 'tensor', axis=0, tiled=True))  88.4 us
    all_gather x1, waiting for transfers between devices, on_device(): gathered = lax.all_gather(normed, 'tensor', axis=0, tiled=True)  81.9 us
    ppermute x7, waiting for transfers between devices, send_pages(): received.append(lax.ppermute(pieces[apart], 'tensor', hops))  47.9 us
    dot_general x2, matrix products, on_device(): jnp.dot(gathers[chunk], up_weight, preferred_element_type=jnp.float32)  32.5 us
    pallas_call x1, Pallas kernels, attend(): pl.pallas_call(functools.partial(attend_kernel, window, seq_len), grid=(s...  18.6 us
    dot_general x2, matrix products, on_device(): terms = jnp.dot(expanded, down_weight, preferred_element_type=jnp.float32)  12.2 us
    unnamed x55, local copies, waits for them, and re-layouts  11.8 us
  transfers between devices with their start and end apart: 14, of which 8 were waited for; matrix products, arithmetic and copies ran while one was open for 14% of the time, Pallas kernels for 0%

profile of v1, /device:TPU:0, one launch (start us, length us, event | category | flops | bytes accessed | tf_op | source)
XLA Modules:
  0.0 534.7 jit_solution(4215924561595695336)
XLA Ops:
  7.3 1.6 convert_reduce_fusion
  8.9 1.6 fusion.22
  10.5 2.7 fusion.25
  13.3 1.4 copy.25.qseg_ref
  15.4 0.1 fusion.41
  15.5 0.2 reduce_window_sum.11
  15.7 0.2 select_reduce_fusion.1
  15.9 0.1 fusion.40
  16.0 0.1 broadcast_in_dim.43
  16.1 0.1 select_reduce_fusion
  16.3 81.9 %all-gather.4.cloned.1.call-done = bf16[2048,2048]{1,0:T(8,128)(2,1)} async-done(((bf16[256,2048]{1,0:T(8,128)(2,1)}), bf16[2048,2048]{1,0:T(8,128)(2,1)}) %all-gather.4.cloned.1.call-update) | async-done | bytes 8388624 | tf_op jit(solution)/shard_map/all_gather | solution.py:155
  98.1 10.2 %add_convert_fusion.q_ref.k_ref.v_ref = bf16[2048,768]{1,0:T(8,128)(2,1)} fusion(f32[768]{0:T(1024)S(1)} %convert_element_type.85, bf16[2048,2048]{1,0:T(8,128)(2,1)} %all-gather.4.cloned.1.call-done, bf16[2048,768]{1,0:T(8,128)(2,1)S(1)} %copy-done), kind=kOutput, calls=%fused_computation.4 | convolution fusion | flops 6445596672 | bytes 14683136 | tf_op jit(solution)/shard_map/dot_general | solution.py:157
  108.3 7.0 %reshape.105 = bf16[2048,2,384]{2,1,0:T(2,128)(2,1)} reshape(bf16[2048,768]{1,0:T(8,128)(2,1)} %add_convert_fusion.q_ref.k_ref.v_ref) | data formatting | bytes 6291456 | tf_op jit(solution)/shard_map/reshape | solution.py:162
  115.3 4.6 slice.24
  119.9 4.4 reshape.106
  124.3 1.2 copy-done.3
  125.5 18.6 %shard_map.167 = bf16[2048,256]{1,0:T(8,128)(2,1)S(1)} custom-call(bf16[2048,768]{1,0:T(8,128)(2,1)S(1)} %copy-done.2, bf16[2048,768]{1,0:T(8,128)(2,1)S(1)} %copy-done.2, bf16[2048,768]{1,0:T(8,128)(2,1)S(1)} %copy-done.2, s32[2048,1]{1,0:T(8,128)S(1)} %copy-done.3, s32[1,1,2048]{2,1,0:T(1,128)S(1)} %bitcast.63), custom_call_target="tpu_custom_call" | custom-call | flops 2684354560 | bytes 6291456 | tf_op jit(solution)/shard_map/pallas_call | solution.py:52
  144.1 1.0 copy-done.4
  145.1 0.4 broadcast_select_fusion.1
  145.5 2.8 gather_fusion
  148.4 2.5 broadcast_select_fusion
  150.9 2.1 dynamic-slice_bitcast_fusion
  153.0 0.1 fusion.42
  153.1 0.7 copy-done.11
  153.7 3.3 convolution_convert_fusion
  157.1 3.2 convolution_convert_fusion.1
  160.4 0.2 all-gather.6.cloned.1.call-start
  160.6 45.1 %reduce-scatter.7.cloned.1.call-done = bf16[128,2048]{1,0:T(8,128)(2,1)} async-done(((bf16[1024,2048]{1,0:T(8,128)(2,1)}), bf16[128,2048]{1,0:T(8,128)(2,1)}) %reduce-scatter.7.cloned.1.call-update) | async-done | bytes 524304 | tf_op jit(solution)/shard_map/reduce_scatter | solution.py:189
  205.7 1.3 convert_reduce_fusion.2
  207.0 0.3 fusion.34
  207.4 1.2 fusion.37
  208.6 47.6 %reduce-scatter.5.cloned.1.call-done = bf16[128,2048]{1,0:T(8,128)(2,1)} async-done(((bf16[1024,2048]{1,0:T(8,128)(2,1)}), bf16[128,2048]{1,0:T(8,128)(2,1)}) %reduce-scatter.5.cloned.1.call-update) | async-done | bytes 524304 | tf_op jit(solution)/shard_map/reduce_scatter | solution.py:189
  256.2 1.3 convert_reduce_fusion.1
  257.5 0.3 fusion.30
  257.8 1.2 fusion.33
  259.1 0.1 collective-permute-start
  259.3 1.8 collective-permute-start.2
  261.1 0.2 collective-permute-start.3
  261.2 2.4 collective-permute-start.4
  263.7 0.7 collective-permute-start.5
  264.4 47.9 %collective-permute-done.1 = bf16[32,16,512]{2,1,0:T(8,128)(2,1)S(1)} collective-permute-done((bf16[32,16,512]{2,1,0:T(8,128)(2,1)}, bf16[32,16,512]{2,1,0:T(8,128)(2,1)S(1)}, u32[]{:S(2)}, u32[]{:S(2)}) %collective-permute-start.1) | collective-permute-done | bytes 524320 | tf_op jit(solution)/shard_map/ppermute | solution.py:114
  312.3 0.5 collective-permute-start.6
  312.8 52.6 %all-gather.6.cloned.1.call-done = bf16[1024,2048]{1,0:T(8,128)(2,1)} async-done(((bf16[128,2048]{1,0:T(8,128)(2,1)}), bf16[1024,2048]{1,0:T(8,128)(2,1)}) %all-gather.6.cloned.1.call-update) | async-done | bytes 4194320 | tf_op jit(solution)/shard_map/all_gather | solution.py:206
  365.5 16.2 %fusion.2 = bf16[1024,1024]{1,0:T(8,128)(2,1)S(1)} fusion(f32[1024]{0:T(1024)S(1)} %copy-done.23, bf16[1024,2048]{1,0:T(8,128)(2,1)} %all-gather.6.cloned.1.call-done, bf16[2048,1024]{1,0:T(8,128)(2,1)} %param.25), kind=kOutput, calls=%fused_computation.7 | convolution fusion | flops 4364173312 | bytes 10489856 | tf_op jit(solution)/shard_map/dot_general | solution.py:209
  381.8 6.1 %convolution_convert_fusion.3 = bf16[1024,2048]{1,0:T(8,128)(2,1)} fusion(bf16[1024,1024]{1,0:T(8,128)(2,1)S(1)} %fusion.2, bf16[1024,2048]{1,0:T(8,128)(2,1)S(1)} %copy-done.21), kind=kOutput, calls=%fused_computation.45 | convolution fusion | flops 4297064448 | bytes 10485760 | tf_op jit(solution)/shard_map/dot_general | solution.py:215
  387.9 0.3 reduce-scatter.11.cloned.1.call-start
  388.2 35.8 %all-gather.8.cloned.1.call-done = bf16[1024,2048]{1,0:T(8,128)(2,1)} async-done(((bf16[128,2048]{1,0:T(8,128)(2,1)}), bf16[1024,2048]{1,0:T(8,128)(2,1)}) %all-gather.8.cloned.1.call-update) | async-done | bytes 4194320 | tf_op jit(solution)/shard_map/all_gather | solution.py:206
  424.0 16.2 %fusion.5 = bf16[1024,1024]{1,0:T(8,128)(2,1)S(1)} fusion(f32[1024]{0:T(1024)S(1)} %copy-done.23, bf16[1024,2048]{1,0:T(8,128)(2,1)} %all-gather.8.cloned.1.call-done, bf16[2048,1024]{1,0:T(8,128)(2,1)} %param.25), kind=kOutput, calls=%fused_computation.10 | convolution fusion | flops 4364173312 | bytes 10489856 | tf_op jit(solution)/shard_map/dot_general | solution.py:209
  440.3 6.1 %convolution_convert_fusion.2 = bf16[1024,2048]{1,0:T(8,128)(2,1)} fusion(bf16[1024,1024]{1,0:T(8,128)(2,1)S(1)} %fusion.5, bf16[1024,2048]{1,0:T(8,128)(2,1)S(1)} %copy-done.22), kind=kOutput, calls=%fused_computation.44 | convolution fusion | flops 4297064448 | bytes 10485760 | tf_op jit(solution)/shard_map/dot_general | solution.py:215
  446.4 1.0 copy-done.12
  447.4 0.8 bitcast_dynamic-update-slice_fusion.7
  448.2 0.8 bitcast_dynamic-update-slice_fusion.6
  449.1 0.8 bitcast_dynamic-update-slice_fusion.5
  449.9 0.8 bitcast_dynamic-update-slice_fusion.4
  450.7 0.8 bitcast_dynamic-update-slice_fusion.3
  451.5 1.9 bitcast_dynamic-update-slice_fusion.2
  453.4 1.9 bitcast_dynamic-update-slice_fusion.1
  455.3 1.9 bitcast_dynamic-update-slice_fusion
  457.2 5.0 gather_fusion.1
  462.2 5.0 copy.28
  467.2 7.1 %reduce-scatter.9.cloned.1.call-done = bf16[128,2048]{1,0:T(8,128)(2,1)} async-done(((bf16[1024,2048]{1,0:T(8,128)(2,1)}), bf16[128,2048]{1,0:T(8,128)(2,1)}) %reduce-scatter.9.cloned.1.call-update) | async-done | bytes 524304 | tf_op jit(solution)/shard_map/reduce_scatter | solution.py:217
  474.4 50.5 %reduce-scatter.11.cloned.1.call-done = bf16[128,2048]{1,0:T(8,128)(2,1)} async-done(((bf16[1024,2048]{1,0:T(8,128)(2,1)}), bf16[128,2048]{1,0:T(8,128)(2,1)}) %reduce-scatter.11.cloned.1.call-update) | async-done | bytes 524304 | tf_op jit(solution)/shard_map/reduce_scatter | solution.py:217
  524.8 1.9 add_convert_fusion.2
  526.8 1.1 pad_maximum_fusion
  (74 shorter events, 0.6 us)
Async XLA Ops:
  7.2 91.0 %copy-start = (bf16[2048,768]{1,0:T(8,128)(2,1)S(1)}, bf16[2048,768]{1,0:T(8,128)(2,1)}, u32[]{:S(2)}) copy-start(bf16[2048,768]{1,0:T(8,128)(2,1)} %param.19) | copy-start | bytes 9437188
  7.2 6.1 %copy-start.20 = (bf16[768]{0:T(1024)(128)(2,1)S(1)}, bf16[768]{0:T(1024)(128)(2,1)}, u32[]{:S(2)}) copy-start(bf16[768]{0:T(1024)(128)(2,1)} %param.20) | copy-start | bytes 4612
  7.2 6.1 %copy-start.6 = (s32[1,2048]{1,0:T(1,128)S(1)}, s32[1,2048]{1,0:T(1,128)}, u32[]{:S(2)}) copy-start(s32[1,2048]{1,0:T(1,128)} %param.29) | copy-start | bytes 24580
  7.2 8.2 %copy-start.19 = (s32[128,1]{0,1:T(1,128)S(1)}, s32[128,1]{0,1:T(1,128)}, u32[]{:S(2)}) copy-start(s32[128,1]{0,1:T(1,128)} %param.31) | copy-start | bytes 1540
  7.2 90.9 %all-gather.4.cloned.1.call-start = ((), (), s32[]{:S(2)}) async-start(), calls=%async_computation.4 | async-start | bytes 9437184 | tf_op jit(solution)/shard_map/all_gather | solution.py:155
  13.2 192.5 %reduce-scatter.7.cloned.1.call-start = ((), (), s32[]{:S(2)}) async-start(), calls=%async_computation.6 | async-start | bytes 4718592 | tf_op jit(solution)/shard_map/reduce_scatter | solution.py:189
  115.3 9.0 %copy-start.2 = (bf16[2048,768]{1,0:T(8,128)(2,1)S(1)}, bf16[2048,768]{1,0:T(8,128)(2,1)}, u32[]{:S(2)}) copy-start(bf16[2048,768]{1,0:T(8,128)(2,1)} %add_convert_fusion.q_ref.k_ref.v_ref) | copy-start | bytes 9437188
  124.3 1.2 copy-start.3
  125.5 19.6 %copy-start.8 = (bf16[128,16,512]{2,1,0:T(8,128)(2,1)S(1)}, bf16[128,16,512]{2,1,0:T(8,128)(2,1)}, u32[]{:S(2)}) copy-start(bf16[128,16,512]{2,1,0:T(8,128)(2,1)} %reshape.106) | copy-start | bytes 6291460
  144.1 1.0 copy-start.4
  150.8 2.1 copy-start.5
  150.9 2.9 copy-start.11
  157.0 99.2 %reduce-scatter.5.cloned.1.call-start = ((), (), s32[]{:S(2)}) async-start(), calls=%async_computation.5 | async-start | bytes 4718592 | tf_op jit(solution)/shard_map/reduce_scatter | solution.py:189
  157.1 48.6 %copy-start.7 = (bf16[256,2048]{1,0:T(8,128)(2,1)S(1)}, bf16[256,2048]{1,0:T(8,128)(2,1)}, u32[]{:S(2)}) copy-start(bf16[256,2048]{1,0:T(8,128)(2,1)} %param.16) | copy-start | bytes 3145732
  157.1 48.6 %copy-start.15 = (f32[2048]{0:T(1024)S(1)}, f32[2048]{0:T(1024)}, u32[]{:S(2)}) copy-start(f32[2048]{0:T(1024)} %param.22) | copy-start | bytes 24580
  160.3 47.0 %copy-start.16 = (f32[2048]{0:T(1024)S(1)}, f32[2048]{0:T(1024)}, u32[]{:S(2)}) copy-start(f32[2048]{0:T(1024)} %param.24) | copy-start | bytes 24580
  160.3 47.0 %copy-start.17 = (f32[2048]{0:T(1024)S(1)}, f32[2048]{0:T(1024)}, u32[]{:S(2)}) copy-start(f32[2048]{0:T(1024)} %param.23) | copy-start | bytes 24580
  160.4 205.1 %copy-start.23 = (f32[1024]{0:T(1024)S(1)}, f32[1024]{0:T(1024)}, u32[]{:S(2)}) copy-start(f32[1024]{0:T(1024)} %param.26) | copy-start | bytes 12292
  160.4 205.1 %all-gather.6.cloned.1.call-start = ((), (), s32[]{:S(2)}) async-start(), calls=%async_computation.7 | async-start | bytes 4718592 | tf_op jit(solution)/shard_map/all_gather | solution.py:206
  207.0 174.7 %copy-start.9 = (bf16[128,2048]{1,0:T(8,128)(2,1)}, bf16[128,2048]{1,0:T(8,128)(2,1)S(1)}, u32[]{:S(2)}) copy-start(bf16[128,2048]{1,0:T(8,128)(2,1)S(1)} %get-tuple-element.23) | copy-start | bytes 1572868
  208.6 215.4 %all-gather.8.cloned.1.call-start = ((), (), s32[]{:S(2)}) async-start(), calls=%async_computation.9 | async-start | bytes 4718592 | tf_op jit(solution)/shard_map/all_gather | solution.py:206
  257.5 124.2 %copy-start.10 = (bf16[128,2048]{1,0:T(8,128)(2,1)}, bf16[128,2048]{1,0:T(8,128)(2,1)S(1)}, u32[]{:S(2)}) copy-start(bf16[128,2048]{1,0:T(8,128)(2,1)S(1)} %get-tuple-element.43) | copy-start | bytes 1572868
  259.1 215.3 %reduce-scatter.9.cloned.1.call-start = ((), (), s32[]{:S(2)}) async-start(), calls=%async_computation.8 | async-start | bytes 4718592 | tf_op jit(solution)/shard_map/reduce_scatter | solution.py:217
  259.1 4.5 collective-permute-start
  259.2 53.1 %collective-permute-start.1 = (bf16[32,16,512]{2,1,0:T(8,128)(2,1)}, bf16[32,16,512]{2,1,0:T(8,128)(2,1)S(1)}, u32[]{:S(2)}, u32[]{:S(2)}) collective-permute-start(bf16[32,16,512]{2,1,0:T(8,128)(2,1)} %get-tuple-element.26), channel_id=1, source_target_pairs={{0,2},{1,3},{2,0},{3,1},{4,6},{5,7},{6,4},{7,5},{8,10},{9,11},{10,... | collective-permute-start | bytes 1572872 | tf_op jit(solution)/shard_map/ppermute | solution.py:114
  259.3 122.5 %collective-permute-start.2 = (bf16[32,16,512]{2,1,0:T(8,128)(2,1)}, bf16[32,16,512]{2,1,0:T(8,128)(2,1)S(1)}, u32[]{:S(2)}, u32[]{:S(2)}) collective-permute-start(bf16[32,16,512]{2,1,0:T(8,128)(2,1)} %get-tuple-element.27), channel_id=1, source_target_pairs={{0,3},{1,2},{2,1},{3,0},{4,7},{5,6},{6,5},{7,4},{8,11},{9,10},{10,... | collective-permute-start | bytes 1572872 | tf_op jit(solution)/shard_map/ppermute | solution.py:114
  261.1 120.7 %collective-permute-start.3 = (bf16[32,16,512]{2,1,0:T(8,128)(2,1)}, bf16[32,16,512]{2,1,0:T(8,128)(2,1)S(1)}, u32[]{:S(2)}, u32[]{:S(2)}) collective-permute-start(bf16[32,16,512]{2,1,0:T(8,128)(2,1)} %get-tuple-element.28), channel_id=1, source_target_pairs={{0,4},{1,5},{2,6},{3,7},{4,0},{5,1},{6,2},{7,3},{8,12},{9,13},{10,... | collective-permute-start | bytes 1572872 | tf_op jit(solution)/shard_map/ppermute | solution.py:114
  261.2 120.5 %collective-permute-start.4 = (bf16[32,16,512]{2,1,0:T(8,128)(2,1)}, bf16[32,16,512]{2,1,0:T(8,128)(2,1)}, u32[]{:S(2)}, u32[]{:S(2)}) collective-permute-start(bf16[32,16,512]{2,1,0:T(8,128)(2,1)} %get-tuple-element.29), channel_id=1, source_target_pairs={{0,5},{1,4},{2,7},{3,6},{4,1},{5,0},{6,3},{7,2},{8,13},{9,12},{10,... | collective-permute-start | bytes 1572872 | tf_op jit(solution)/shard_map/ppermute | solution.py:114
  263.7 118.1 %collective-permute-start.5 = (bf16[32,16,512]{2,1,0:T(8,128)(2,1)}, bf16[32,16,512]{2,1,0:T(8,128)(2,1)}, u32[]{:S(2)}, u32[]{:S(2)}) collective-permute-start(bf16[32,16,512]{2,1,0:T(8,128)(2,1)} %get-tuple-element.30), channel_id=1, source_target_pairs={{0,6},{1,7},{2,4},{3,5},{4,2},{5,3},{6,0},{7,1},{8,14},{9,15},{10,... | collective-permute-start | bytes 1572872 | tf_op jit(solution)/shard_map/ppermute | solution.py:114
  312.3 69.5 %collective-permute-start.6 = (bf16[32,16,512]{2,1,0:T(8,128)(2,1)}, bf16[32,16,512]{2,1,0:T(8,128)(2,1)}, u32[]{:S(2)}, u32[]{:S(2)}) collective-permute-start(bf16[32,16,512]{2,1,0:T(8,128)(2,1)} %get-tuple-element.31), channel_id=1, source_target_pairs={{0,7},{1,6},{2,5},{3,4},{4,3},{5,2},{6,1},{7,0},{8,15},{9,14},{10,... | collective-permute-start | bytes 1572872 | tf_op jit(solution)/shard_map/ppermute | solution.py:114
  365.5 16.3 %copy-start.21 = (bf16[1024,2048]{1,0:T(8,128)(2,1)S(1)}, bf16[1024,2048]{1,0:T(8,128)(2,1)}, u32[]{:S(2)}) copy-start(bf16[1024,2048]{1,0:T(8,128)(2,1)} %param.27) | copy-start | bytes 12582916
  381.8 6.2 %copy-start.13 = (bf16[32,16,512]{2,1,0:T(8,128)(2,1)}, bf16[32,16,512]{2,1,0:T(8,128)(2,1)S(1)}, u32[]{:S(2)}) copy-start(bf16[32,16,512]{2,1,0:T(8,128)(2,1)S(1)} %collective-permute-done.3) | copy-start | bytes 1572868
  387.9 136.9 %reduce-scatter.11.cloned.1.call-start = ((), (), s32[]{:S(2)}) async-start(), calls=%async_computation.10 | async-start | bytes 4718592 | tf_op jit(solution)/shard_map/reduce_scatter | solution.py:217
  424.0 16.2 %copy-start.22 = (bf16[1024,2048]{1,0:T(8,128)(2,1)S(1)}, bf16[1024,2048]{1,0:T(8,128)(2,1)}, u32[]{:S(2)}) copy-start(bf16[1024,2048]{1,0:T(8,128)(2,1)} %param.27) | copy-start | bytes 12582916
  446.4 1.0 copy-start.12
  446.4 4.4 copy-start.14
  462.2 62.7 %copy-start.18 = (f32[2048]{0:T(1024)S(1)}, f32[2048]{0:T(1024)}, u32[]{:S(2)}) copy-start(f32[2048]{0:T(1024)} %param.28) | copy-start | bytes 24580
  462.2 65.7 %copy-start.1 = (bf16[2048,768]{1,0:T(8,128)(2,1)S(1)}, bf16[2048,768]{1,0:T(8,128)(2,1)}, u32[]{:S(2)}) copy-start(bf16[2048,768]{1,0:T(8,128)(2,1)} %param.19) | copy-start | bytes 9437188
Sparse Core Ops, SparseCore 0:
  13.3 84.7 all-gather.3
  157.2 48.5 reduce-scatter.6
  208.0 48.1 reduce-scatter.4
  258.2 107.1 all-gather.5
  367.5 56.4 all-gather.7
  426.2 48.1 reduce-scatter.8
  476.6 48.1 reduce-scatter.10

commit v2 on v1

--- a/solution.py
+++ b/solution.py
@@ -84,24 +84,25 @@
     return jnp.concatenate([first, second], axis=axis)
 
 
-def pack_pages(page_rows, page_table, capacity, position):
+def pack_pages(keys_vals, live, page_table, capacity, position):
     devices = lax.axis_size("tensor")
-    pages = page_rows.shape[0]
+    pages = keys_vals.shape[0] // PAGE
     owners = page_table[:, 0]
     onehot = (owners[:, None] == jnp.arange(devices, dtype=jnp.int32)[None, :]).astype(jnp.int32)
     ranks = jnp.sum((jnp.cumsum(onehot, axis=0) - onehot) * onehot, axis=1)
     slot_ids = owners * capacity + ranks
-    hits = slot_ids[None, :] == jnp.arange(devices * capacity, dtype=jnp.int32)[:, None]
-    taken = jnp.any(hits, axis=1)
-    source_page = jnp.sum(
-        jnp.where(hits, jnp.arange(pages, dtype=jnp.int32)[None, :], 0), axis=1
-    )
-    outgoing = jnp.where(
-        taken[:, None, None], jnp.take(page_rows, source_page, axis=0, mode="clip"), 0
-    ).astype(jnp.bfloat16)
-    outgoing = outgoing.reshape((devices, capacity) + page_rows.shape[1:])
+    owner_order = position ^ jnp.arange(devices, dtype=jnp.int32)
+    slots = owner_order[:, None] * capacity + jnp.arange(capacity, dtype=jnp.int32)[None, :]
+    hits = slot_ids[None, :] == slots.reshape(-1)[:, None]
+    numbers = jnp.arange(pages, dtype=jnp.int32)
+    source_page = jnp.sum(jnp.where(hits, numbers[None, :], 0), axis=1)
+    live_pages = live.reshape(pages, PAGE).astype(jnp.int32)
+    kept = jnp.sum(jnp.where(hits[:, :, None], live_pages[None], 0), axis=1) > 0
+    page_rows = keys_vals.reshape(pages, PAGE, -1)
+    taken = jnp.take(page_rows, source_page, axis=0, mode="clip")
+    outgoing = jnp.where(kept[:, :, None], taken, 0).astype(jnp.bfloat16)
     return [
-        lax.dynamic_index_in_dim(outgoing, position ^ apart, 0, keepdims=False)
+        lax.slice_in_dim(outgoing, apart * capacity, (apart + 1) * capacity, axis=0)
         for apart in range(devices)
     ]
 
@@ -158,26 +159,30 @@
         + qkv_bias.astype(jnp.float32)
     ).astype(jnp.bfloat16)
     heads_here = projected.shape[1] // (3 * HD)
+    keys_vals = jnp.concatenate(
+        [
+            lax.slice_in_dim(projected, (3 * n + 1) * HD, (3 * n + 3) * HD, axis=1)
+            for n in range(heads_here)
+        ],
+        axis=1,
+    )
+    if not whole_heads:
+        half = keys_vals.shape[1] // 2
+        keys_vals = lax.dynamic_slice_in_dim(keys_vals, position % 2 * half, half, 1)
+    live = jnp.arange(seq_len, dtype=jnp.int32)[None, :] < prompt_lengths[:, None]
+    pieces = pack_pages(
+        keys_vals, live, page_table, 2 * (total_rows // PAGE) // devices, position
+    )
+    projected, pieces = lax.optimization_barrier((projected, pieces))
+    received = send_pages(pieces)
+    far, step = devices // 2, devices // 8
     attended = attend(projected, segment_ids)
-    keys_vals = projected.reshape(total_rows, heads_here, 3 * HD)[:, :, HD:]
-    keys_vals = keys_vals.reshape(total_rows, heads_here * 2 * HD)
     if not whole_heads:
         half = attended.shape[1] // 2
         attended = lax.dynamic_slice_in_dim(attended, position % 2 * half, half, 1)
-        half = keys_vals.shape[1] // 2
-        keys_vals = lax.dynamic_slice_in_dim(keys_vals, position % 2 * half, half, 1)
-
-    blocks_total = total_rows // PAGE
-    live = jnp.arange(seq_len, dtype=jnp.int32)[None, :] < prompt_lengths[:, None]
-    kept_rows = jnp.where(live.reshape(total_rows, 1), keys_vals, 0).astype(jnp.bfloat16)
-    pieces = pack_pages(
-        kept_rows.reshape(blocks_total, PAGE, -1),
-        page_table,
-        2 * blocks_total // devices,
-        position,
-    )
-    attended, pieces = lax.optimization_barrier((attended, pieces))
-    received = send_pages(pieces)
+    attended, received[far : far + step] = lax.optimization_barrier(
+        (attended, received[far : far + step])
+    )
 
     part = tok_rows // CHUNKS
     shaped = attended.reshape(devices, CHUNKS, part, attended.shape[1])
@@ -194,9 +199,13 @@
     for chunk in range(CHUNKS):
         hidden = lax.slice_in_dim(hidden_in, chunk * part, (chunk + 1) * part, axis=0)
         attn_sum = sums[chunk]
-        if chunk > 0:
-            attn_sum, residuals[-1], _ = lax.optimization_barrier(
-                (attn_sum, residuals[-1], normed_mid)
+        if chunk == 0:
+            attn_sum, received[far + step : far + 3 * step] = lax.optimization_barrier(
+                (attn_sum, received[far + step : far + 3 * step])
+            )
+        else:
+            attn_sum, residuals[-1], received, _ = lax.optimization_barrier(
+                (attn_sum, residuals[-1], received, normed_mid)
             )
         residual_mid = (
             hidden.astype(jnp.float32) + attn_sum.astype(jnp.float32) + out_bias
@@ -208,10 +217,7 @@
     for chunk in range(CHUNKS):
         lifted = jnp.dot(gathers[chunk], up_weight, preferred_element_type=jnp.float32) + up_bias
         expanded = jax.nn.gelu(lifted, approximate=False).astype(jnp.bfloat16)
-        if chunk == 0:
-            expanded, received = lax.optimization_barrier((expanded, received))
-        else:
-            expanded = lax.optimization_barrier(expanded)
+        expanded = lax.optimization_barrier(expanded)
         terms = jnp.dot(expanded, down_weight, preferred_element_type=jnp.float32)
         sums.append(
             lax.psum_scatter(

time: 535 us -> 526 us (0.983)
  local copies, waits for them, and re-layouts: 46.3 us -> 32.8 us
    ppermute x7, waiting for transfers between devices: 47.9 us -> 119 us  [send_pages(): received.append(lax.ppermute(pieces[apart], 'tensor', hops))]
    reduce_scatter x4, waiting for transfers between devices: 150 us -> 97.1 us  [on_device(): lax.psum_scatter(terms.astype(jnp.bfloat16), 'tensor', scatter_dimension=...]
    all_gather x2, waiting for transfers between devices: 88.4 us -> 70.3 us  [on_device(): gathers.append(lax.all_gather(normed_mid, 'tensor', axis=0, tiled=True))]
    reshape x2 -> x0, local copies, waits for them, and re-layouts: 11.4 us -> none  [the longest x1 7.02 us: on_device(): keys_vals = projected.reshape(total_rows, heads_here, 3 * HD)[:, :, HD:]]
    unnamed x55 -> x69, local copies, waits for them, and re-layouts: 11.8 us -> 14.2 us
  transfers between devices with their start and end apart: 14 -> 14, of which waited for: 8 -> 12; matrix products, arithmetic and copies ran while one was open for 14% -> 15% of each run, Pallas kernels for 0% -> 4%
where the time goes in v2:
time: 526 us
  waiting for transfers between devices  365 us (69%)
  matrix products  60.2 us (11%)
  local copies, waits for them, and re-layouts  32.8 us (6%)
  other arithmetic  22.5 us (4%)
  Pallas kernels  18.6 us (4%)
  between operations  15.2 us (3%)
  starting transfers between devices  11 us (2%)
    ppermute x7, waiting for transfers between devices, send_pages(): received.append(lax.ppermute(pieces[apart], 'tensor', hops))  119 us
    reduce_scatter x4, waiting for transfers between devices, on_device(): lax.psum_scatter(terms.astype(jnp.bfloat16), 'tensor', scatter_dimension=...  97.1 us
    all_gather x1, waiting for transfers between devices, on_device(): gathered = lax.all_gather(normed, 'tensor', axis=0, tiled=True)  78.8 us
    all_gather x2, waiting for transfers between devices, on_device(): gathers.append(lax.all_gather(normed_mid, 'tensor', axis=0, tiled=True))  70.3 us
    dot_general x2, matrix products, on_device(): jnp.dot(gathers[chunk], up_weight, preferred_element_type=jnp.float32)  32.5 us
    pallas_call x1, Pallas kernels, attend(): pl.pallas_call(functools.partial(attend_kernel, window, seq_len), grid=(s...  18.6 us
    unnamed x69, local copies, waits for them, and re-layouts  14.2 us
    dot_general x2, matrix products, on_device(): terms = jnp.dot(expanded, down_weight, preferred_element_type=jnp.float32)  12.3 us
  transfers between devices with their start and end apart: 14, of which 12 were waited for; matrix products, arithmetic and copies ran while one was open for 15% of the time, Pallas kernels for 4%

profile of v2, /device:TPU:0, one launch (start us, length us, event | category | flops | bytes accessed | tf_op | source)
XLA Modules:
  0.0 525.5 jit_solution(12005943282517243672)
XLA Ops:
  7.2 1.6 convert_reduce_fusion
  8.9 1.6 fusion.22
  10.5 2.7 fusion.25
  14.2 0.2 reduce_window_sum.11
  14.4 0.2 select_reduce_fusion.2
  14.6 0.2 select_reduce_fusion.1
  14.8 0.1 broadcast_compare_fusion.1
  14.9 4.4 select_reduce_fusion
  19.3 78.8 %all-gather.4.cloned.1.call-done = bf16[2048,2048]{1,0:T(8,128)(2,1)} async-done(((bf16[256,2048]{1,0:T(8,128)(2,1)}), bf16[2048,2048]{1,0:T(8,128)(2,1)}) %all-gather.4.cloned.1.call-update) | async-done | bytes 8388624 | tf_op jit(solution)/shard_map/all_gather | solution.py:156
  98.1 9.0 %add_convert_fusion.q_ref.k_ref.v_ref = bf16[2048,768]{1,0:T(8,128)(2,1)S(1)} fusion(f32[768]{0:T(1024)S(1)} %convert_element_type.90, bf16[2048,2048]{1,0:T(8,128)(2,1)} %all-gather.4.cloned.1.call-done, bf16[2048,768]{1,0:T(8,128)(2,1)S(1)} %copy-done), kind=kOutput, calls=%fused_computation.4 | convolution fusion | flops 6445596672 | bytes 14683136 | tf_op jit(solution)/shard_map/dot_general | solution.py:158
  107.2 0.1 fusion.43
  107.3 0.2 pad_maximum_fusion
  107.5 1.3 copy-done.2
  108.8 2.8 gather_fusion
  111.6 2.6 broadcast_select_fusion
  114.3 2.2 fusion.42
  116.4 0.9 collective-permute-start
  117.4 1.3 copy.24.qseg_ref
  118.7 1.2 copy-done.4
  120.0 18.6 %shard_map.167 = bf16[2048,256]{1,0:T(8,128)(2,1)S(1)} custom-call(bf16[2048,768]{1,0:T(8,128)(2,1)S(1)} %copy-done.3, bf16[2048,768]{1,0:T(8,128)(2,1)S(1)} %copy-done.3, bf16[2048,768]{1,0:T(8,128)(2,1)S(1)} %copy-done.3, s32[2048,1]{1,0:T(8,128)S(1)} %copy-done.4, s32[1,1,2048]{2,1,0:T(1,128)S(1)} %bitcast.47), custom_call_target="tpu_custom_call" | custom-call | flops 2684354560 | bytes 6291456 | tf_op jit(solution)/shard_map/pallas_call | solution.py:52
  138.5 2.7 collective-permute-done
  141.3 3.3 convolution_convert_fusion
  144.7 0.2 reduce-scatter.5.cloned.1.call-start
  144.9 3.2 convolution_convert_fusion.1
  148.3 0.8 copy-done.15
  149.2 2.3 collective-permute-start.2
  151.5 53.3 %collective-permute-done.1 = bf16[32,16,512]{2,1,0:T(8,128)(2,1)} collective-permute-done((bf16[32,16,512]{2,1,0:T(8,128)(2,1)}, bf16[32,16,512]{2,1,0:T(8,128)(2,1)}, u32[]{:S(2)}, u32[]{:S(2)}) %collective-permute-start.1) | collective-permute-done | bytes 524320 | tf_op jit(solution)/shard_map/ppermute | solution.py:115
  204.7 28.3 %reduce-scatter.7.cloned.1.call-done = bf16[128,2048]{1,0:T(8,128)(2,1)} async-done(((bf16[1024,2048]{1,0:T(8,128)(2,1)}), bf16[128,2048]{1,0:T(8,128)(2,1)}) %reduce-scatter.7.cloned.1.call-update) | async-done | bytes 524304 | tf_op jit(solution)/shard_map/reduce_scatter | solution.py:194
  233.0 1.3 convert_reduce_fusion.2
  234.3 0.3 fusion.34
  234.7 1.2 fusion.37
  235.9 2.5 collective-permute-start.3
  238.4 2.9 collective-permute-start.4
  241.3 1.7 collective-permute-start.6
  243.0 19.5 %collective-permute-done.4 = bf16[32,16,512]{2,1,0:T(8,128)(2,1)S(1)} collective-permute-done((bf16[32,16,512]{2,1,0:T(8,128)(2,1)S(1)}, bf16[32,16,512]{2,1,0:T(8,128)(2,1)S(1)}, u32[]{:S(2)}, u32[]{:S(2)}) %collective-permute-start.4) | collective-permute-done | bytes 524320 | tf_op jit(solution)/shard_map/ppermute | solution.py:115
  262.5 22.5 %collective-permute-done.5 = bf16[32,16,512]{2,1,0:T(8,128)(2,1)S(1)} collective-permute-done((bf16[32,16,512]{2,1,0:T(8,128)(2,1)S(1)}, bf16[32,16,512]{2,1,0:T(8,128)(2,1)S(1)}, u32[]{:S(2)}, u32[]{:S(2)}) %collective-permute-start.5) | collective-permute-done | bytes 524320 | tf_op jit(solution)/shard_map/ppermute | solution.py:115
  284.9 0.8 copy-done.20
  285.7 20.8 %collective-permute-done.6 = bf16[32,16,512]{2,1,0:T(8,128)(2,1)} collective-permute-done((bf16[32,16,512]{2,1,0:T(8,128)(2,1)S(1)}, bf16[32,16,512]{2,1,0:T(8,128)(2,1)}, u32[]{:S(2)}, u32[]{:S(2)}) %collective-permute-start.6) | collective-permute-done | bytes 524320 | tf_op jit(solution)/shard_map/ppermute | solution.py:115
  306.5 11.7 %reduce-scatter.5.cloned.1.call-done = bf16[128,2048]{1,0:T(8,128)(2,1)} async-done(((bf16[1024,2048]{1,0:T(8,128)(2,1)}), bf16[128,2048]{1,0:T(8,128)(2,1)}) %reduce-scatter.5.cloned.1.call-update) | async-done | bytes 524304 | tf_op jit(solution)/shard_map/reduce_scatter | solution.py:194
  318.3 1.3 convert_reduce_fusion.1
  319.6 0.3 fusion.30
  319.9 1.2 fusion.33
  321.2 45.2 %all-gather.6.cloned.1.call-done = bf16[1024,2048]{1,0:T(8,128)(2,1)} async-done(((bf16[128,2048]{1,0:T(8,128)(2,1)}), bf16[1024,2048]{1,0:T(8,128)(2,1)}) %all-gather.6.cloned.1.call-update) | async-done | bytes 4194320 | tf_op jit(solution)/shard_map/all_gather | solution.py:215
  366.3 16.2 %fusion.2 = bf16[1024,1024]{1,0:T(8,128)(2,1)S(1)} fusion(f32[1024]{0:T(1024)S(1)} %copy-done.30, bf16[1024,2048]{1,0:T(8,128)(2,1)} %all-gather.6.cloned.1.call-done, bf16[2048,1024]{1,0:T(8,128)(2,1)} %param.25), kind=kOutput, calls=%fused_computation.7 | convolution fusion | flops 4364173312 | bytes 10489856 | tf_op jit(solution)/shard_map/dot_general | solution.py:218
  382.6 6.1 %convolution_convert_fusion.3 = bf16[1024,2048]{1,0:T(8,128)(2,1)} fusion(bf16[1024,1024]{1,0:T(8,128)(2,1)S(1)} %fusion.2, bf16[1024,2048]{1,0:T(8,128)(2,1)S(1)} %copy-done.28), kind=kOutput, calls=%fused_computation.45 | convolution fusion | flops 4297064448 | bytes 10485760 | tf_op jit(solution)/shard_map/dot_general | solution.py:221
  388.7 0.3 reduce-scatter.11.cloned.1.call-start
  389.0 25.1 %all-gather.8.cloned.1.call-done = bf16[1024,2048]{1,0:T(8,128)(2,1)} async-done(((bf16[128,2048]{1,0:T(8,128)(2,1)}), bf16[1024,2048]{1,0:T(8,128)(2,1)}) %all-gather.8.cloned.1.call-update) | async-done | bytes 4194320 | tf_op jit(solution)/shard_map/all_gather | solution.py:215
  414.1 16.2 %fusion.5 = bf16[1024,1024]{1,0:T(8,128)(2,1)S(1)} fusion(f32[1024]{0:T(1024)S(1)} %copy-done.30, bf16[1024,2048]{1,0:T(8,128)(2,1)} %all-gather.8.cloned.1.call-done, bf16[2048,1024]{1,0:T(8,128)(2,1)} %param.25), kind=kOutput, calls=%fused_computation.10 | convolution fusion | flops 4364173312 | bytes 10489856 | tf_op jit(solution)/shard_map/dot_general | solution.py:218
  430.4 6.2 %convolution_convert_fusion.2 = bf16[1024,2048]{1,0:T(8,128)(2,1)} fusion(bf16[1024,1024]{1,0:T(8,128)(2,1)S(1)} %fusion.5, bf16[1024,2048]{1,0:T(8,128)(2,1)S(1)} %copy-done.29), kind=kOutput, calls=%fused_computation.44 | convolution fusion | flops 4297064448 | bytes 10485760 | tf_op jit(solution)/shard_map/dot_general | solution.py:221
  436.6 1.0 copy-done.11
  437.6 0.8 bitcast_dynamic-update-slice_fusion.7
  438.4 0.8 bitcast_dynamic-update-slice_fusion.6
  439.3 0.8 bitcast_dynamic-update-slice_fusion.5
  440.1 0.8 bitcast_dynamic-update-slice_fusion.4
  440.9 1.9 bitcast_dynamic-update-slice_fusion.3
  442.8 1.9 bitcast_dynamic-update-slice_fusion.2
  444.7 1.9 bitcast_dynamic-update-slice_fusion.1
  446.6 1.9 bitcast_dynamic-update-slice_fusion
  448.4 5.0 gather_fusion.1
  453.5 5.0 copy.27
  458.5 6.7 %reduce-scatter.9.cloned.1.call-done = bf16[128,2048]{1,0:T(8,128)(2,1)} async-done(((bf16[1024,2048]{1,0:T(8,128)(2,1)}), bf16[128,2048]{1,0:T(8,128)(2,1)}) %reduce-scatter.9.cloned.1.call-update) | async-done | bytes 524304 | tf_op jit(solution)/shard_map/reduce_scatter | solution.py:223
  465.2 50.5 %reduce-scatter.11.cloned.1.call-done = bf16[128,2048]{1,0:T(8,128)(2,1)} async-done(((bf16[1024,2048]{1,0:T(8,128)(2,1)}), bf16[128,2048]{1,0:T(8,128)(2,1)}) %reduce-scatter.11.cloned.1.call-update) | async-done | bytes 524304 | tf_op jit(solution)/shard_map/reduce_scatter | solution.py:223
  515.7 1.9 add_convert_fusion.2
  517.6 1.1 pad_maximum_fusion.1
  (90 shorter events, 0.9 us)
Async XLA Ops:
  7.2 91.0 %copy-start = (bf16[2048,768]{1,0:T(8,128)(2,1)S(1)}, bf16[2048,768]{1,0:T(8,128)(2,1)}, u32[]{:S(2)}) copy-start(bf16[2048,768]{1,0:T(8,128)(2,1)} %param.19) | copy-start | bytes 9437188
  7.2 6.1 %copy-start.27 = (bf16[768]{0:T(1024)(128)(2,1)S(1)}, bf16[768]{0:T(1024)(128)(2,1)}, u32[]{:S(2)}) copy-start(bf16[768]{0:T(1024)(128)(2,1)} %param.20) | copy-start | bytes 4612
  7.2 6.9 %copy-start.26 = (s32[128,1]{0,1:T(1,128)S(1)}, s32[128,1]{0,1:T(1,128)}, u32[]{:S(2)}) copy-start(s32[128,1]{0,1:T(1,128)} %param.31) | copy-start | bytes 1540
  7.2 90.9 %all-gather.4.cloned.1.call-start = ((), (), s32[]{:S(2)}) async-start(), calls=%async_computation.4 | async-start | bytes 9437184 | tf_op jit(solution)/shard_map/all_gather | solution.py:156
  13.2 219.8 %reduce-scatter.7.cloned.1.call-start = ((), (), s32[]{:S(2)}) async-start(), calls=%async_computation.6 | async-start | bytes 4718592 | tf_op jit(solution)/shard_map/reduce_scatter | solution.py:194
  107.2 1.6 copy-start.2
  114.2 3.1 copy-start.5
  114.2 4.5 copy-start.3
  116.4 24.8 %collective-permute-start = (bf16[32,16,512]{2,1,0:T(8,128)(2,1)}, bf16[32,16,512]{2,1,0:T(8,128)(2,1)}, u32[]{:S(2)}, u32[]{:S(2)}) collective-permute-start(bf16[32,16,512]{2,1,0:T(8,128)(2,1)} %get-tuple-element.27), channel_id=1, source_target_pairs={{0,4},{1,5},{2,6},{3,7},{4,0},{5,1},{6,2},{7,3},{8,12},{9,13},{10,... | collective-permute-start | bytes 1572872 | tf_op jit(solution)/shard_map/ppermute | solution.py:115
  118.7 1.2 copy-start.4
  119.9 21.4 %copy-start.9 = (bf16[256,2048]{1,0:T(8,128)(2,1)S(1)}, bf16[256,2048]{1,0:T(8,128)(2,1)}, u32[]{:S(2)}) copy-start(bf16[256,2048]{1,0:T(8,128)(2,1)} %param.21) | copy-start | bytes 3145732
  141.3 3.5 copy-start.10
  144.7 173.6 %reduce-scatter.5.cloned.1.call-start = ((), (), s32[]{:S(2)}) async-start(), calls=%async_computation.5 | async-start | bytes 4718592 | tf_op jit(solution)/shard_map/reduce_scatter | solution.py:194
  144.9 88.1 %copy-start.6 = (bf16[256,2048]{1,0:T(8,128)(2,1)S(1)}, bf16[256,2048]{1,0:T(8,128)(2,1)}, u32[]{:S(2)}) copy-start(bf16[256,2048]{1,0:T(8,128)(2,1)} %param.16) | copy-start | bytes 3145732
  144.9 88.1 %copy-start.22 = (f32[2048]{0:T(1024)S(1)}, f32[2048]{0:T(1024)}, u32[]{:S(2)}) copy-start(f32[2048]{0:T(1024)} %param.22) | copy-start | bytes 24580
  148.1 1.0 copy-start.15
  148.1 86.5 %copy-start.23 = (f32[2048]{0:T(1024)S(1)}, f32[2048]{0:T(1024)}, u32[]{:S(2)}) copy-start(f32[2048]{0:T(1024)} %param.24) | copy-start | bytes 24580
  148.1 86.5 %copy-start.24 = (f32[2048]{0:T(1024)S(1)}, f32[2048]{0:T(1024)}, u32[]{:S(2)}) copy-start(f32[2048]{0:T(1024)} %param.23) | copy-start | bytes 24580
  148.1 90.3 %copy-start.14 = (bf16[32,16,512]{2,1,0:T(8,128)(2,1)S(1)}, bf16[32,16,512]{2,1,0:T(8,128)(2,1)}, u32[]{:S(2)}) copy-start(bf16[32,16,512]{2,1,0:T(8,128)(2,1)} %get-tuple-element.34) | copy-start | bytes 1572868
  148.1 93.1 %copy-start.13 = (bf16[32,16,512]{2,1,0:T(8,128)(2,1)S(1)}, bf16[32,16,512]{2,1,0:T(8,128)(2,1)}, u32[]{:S(2)}) copy-start(bf16[32,16,512]{2,1,0:T(8,128)(2,1)} %get-tuple-element.35) | copy-start | bytes 1572868
  148.1 93.1 %copy-start.12 = (bf16[32,16,512]{2,1,0:T(8,128)(2,1)S(1)}, bf16[32,16,512]{2,1,0:T(8,128)(2,1)}, u32[]{:S(2)}) copy-start(bf16[32,16,512]{2,1,0:T(8,128)(2,1)} %get-tuple-element.39) | copy-start | bytes 1572868
  148.2 218.2 %copy-start.30 = (f32[1024]{0:T(1024)S(1)}, f32[1024]{0:T(1024)}, u32[]{:S(2)}) copy-start(f32[1024]{0:T(1024)} %param.26) | copy-start | bytes 12292
  148.2 218.2 %all-gather.6.cloned.1.call-start = ((), (), s32[]{:S(2)}) async-start(), calls=%async_computation.7 | async-start | bytes 4718592 | tf_op jit(solution)/shard_map/all_gather | solution.py:215
  148.2 56.5 %collective-permute-start.1 = (bf16[32,16,512]{2,1,0:T(8,128)(2,1)}, bf16[32,16,512]{2,1,0:T(8,128)(2,1)}, u32[]{:S(2)}, u32[]{:S(2)}) collective-permute-start(bf16[32,16,512]{2,1,0:T(8,128)(2,1)} %get-tuple-element.29), channel_id=1, source_target_pairs={{0,5},{1,4},{2,7},{3,6},{4,1},{5,0},{6,3},{7,2},{8,13},{9,12},{10,... | collective-permute-start | bytes 1572872 | tf_op jit(solution)/shard_map/ppermute | solution.py:115
  149.2 55.6 %collective-permute-start.2 = (bf16[32,16,512]{2,1,0:T(8,128)(2,1)S(1)}, bf16[32,16,512]{2,1,0:T(8,128)(2,1)}, u32[]{:S(2)}, u32[]{:S(2)}) collective-permute-start(bf16[32,16,512]{2,1,0:T(8,128)(2,1)S(1)} %copy-done.15), channel_id=1, source_target_pairs={{0,6},{1,7},{2,4},{3,5},{4,2},{5,3},{6,0},{7,1},{8,14},{9,15},{10,... | collective-permute-start | bytes 1572872 | tf_op jit(solution)/shard_map/ppermute | solution.py:115
  234.3 148.3 %copy-start.7 = (bf16[128,2048]{1,0:T(8,128)(2,1)}, bf16[128,2048]{1,0:T(8,128)(2,1)S(1)}, u32[]{:S(2)}) copy-start(bf16[128,2048]{1,0:T(8,128)(2,1)S(1)} %get-tuple-element.40) | copy-start | bytes 1572868
  235.9 178.2 %all-gather.8.cloned.1.call-start = ((), (), s32[]{:S(2)}) async-start(), calls=%async_computation.9 | async-start | bytes 4718592 | tf_op jit(solution)/shard_map/all_gather | solution.py:215
  235.9 7.0 %collective-permute-start.3 = (bf16[32,16,512]{2,1,0:T(8,128)(2,1)}, bf16[32,16,512]{2,1,0:T(8,128)(2,1)S(1)}, u32[]{:S(2)}, u32[]{:S(2)}) collective-permute-start(bf16[32,16,512]{2,1,0:T(8,128)(2,1)} %get-tuple-element.33), channel_id=1, source_target_pairs={{0,1},{1,0},{2,3},{3,2},{4,5},{5,4},{6,7},{7,6},{8,9},{9,8},{10,11... | collective-permute-start | bytes 1572872 | tf_op jit(solution)/shard_map/ppermute | solution.py:115
  238.4 24.1 %collective-permute-start.4 = (bf16[32,16,512]{2,1,0:T(8,128)(2,1)S(1)}, bf16[32,16,512]{2,1,0:T(8,128)(2,1)S(1)}, u32[]{:S(2)}, u32[]{:S(2)}) collective-permute-start(bf16[32,16,512]{2,1,0:T(8,128)(2,1)S(1)} %copy-done.14), channel_id=1, source_target_pairs={{0,2},{1,3},{2,0},{3,1},{4,6},{5,7},{6,4},{7,5},{8,10},{9,11},{10,... | collective-permute-start | bytes 1572872 | tf_op jit(solution)/shard_map/ppermute | solution.py:115
  241.3 43.7 %collective-permute-start.5 = (bf16[32,16,512]{2,1,0:T(8,128)(2,1)S(1)}, bf16[32,16,512]{2,1,0:T(8,128)(2,1)S(1)}, u32[]{:S(2)}, u32[]{:S(2)}) collective-permute-start(bf16[32,16,512]{2,1,0:T(8,128)(2,1)S(1)} %copy-done.13), channel_id=1, source_target_pairs={{0,3},{1,2},{2,1},{3,0},{4,7},{5,6},{6,5},{7,4},{8,11},{9,10},{10,... | collective-permute-start | bytes 1572872 | tf_op jit(solution)/shard_map/ppermute | solution.py:115
  241.3 65.3 %collective-permute-start.6 = (bf16[32,16,512]{2,1,0:T(8,128)(2,1)S(1)}, bf16[32,16,512]{2,1,0:T(8,128)(2,1)}, u32[]{:S(2)}, u32[]{:S(2)}) collective-permute-start(bf16[32,16,512]{2,1,0:T(8,128)(2,1)S(1)} %copy-done.12), channel_id=1, source_target_pairs={{0,7},{1,6},{2,5},{3,4},{4,3},{5,2},{6,1},{7,0},{8,15},{9,14},{10,... | collective-permute-start | bytes 1572872 | tf_op jit(solution)/shard_map/ppermute | solution.py:115
  243.0 42.0 %copy-start.16 = (bf16[32,16,512]{2,1,0:T(8,128)(2,1)}, bf16[32,16,512]{2,1,0:T(8,128)(2,1)S(1)}, u32[]{:S(2)}) copy-start(bf16[32,16,512]{2,1,0:T(8,128)(2,1)S(1)} %collective-permute-done.3) | copy-start | bytes 1572868
  262.5 22.5 %copy-start.18 = (bf16[32,16,512]{2,1,0:T(8,128)(2,1)}, bf16[32,16,512]{2,1,0:T(8,128)(2,1)S(1)}, u32[]{:S(2)}) copy-start(bf16[32,16,512]{2,1,0:T(8,128)(2,1)S(1)} %collective-permute-done.4) | copy-start | bytes 1572868
  284.9 0.8 copy-start.20
  319.6 63.0 %copy-start.8 = (bf16[128,2048]{1,0:T(8,128)(2,1)}, bf16[128,2048]{1,0:T(8,128)(2,1)S(1)}, u32[]{:S(2)}) copy-start(bf16[128,2048]{1,0:T(8,128)(2,1)S(1)} %get-tuple-element.51) | copy-start | bytes 1572868
  321.1 144.1 %reduce-scatter.9.cloned.1.call-start = ((), (), s32[]{:S(2)}) async-start(), calls=%async_computation.8 | async-start | bytes 4718592 | tf_op jit(solution)/shard_map/reduce_scatter | solution.py:223
  366.3 16.3 %copy-start.28 = (bf16[1024,2048]{1,0:T(8,128)(2,1)S(1)}, bf16[1024,2048]{1,0:T(8,128)(2,1)}, u32[]{:S(2)}) copy-start(bf16[1024,2048]{1,0:T(8,128)(2,1)} %param.27) | copy-start | bytes 12582916
  388.7 126.9 %reduce-scatter.11.cloned.1.call-start = ((), (), s32[]{:S(2)}) async-start(), calls=%async_computation.10 | async-start | bytes 4718592 | tf_op jit(solution)/shard_map/reduce_scatter | solution.py:223
  414.1 16.2 %copy-start.29 = (bf16[1024,2048]{1,0:T(8,128)(2,1)S(1)}, bf16[1024,2048]{1,0:T(8,128)(2,1)}, u32[]{:S(2)}) copy-start(bf16[1024,2048]{1,0:T(8,128)(2,1)} %param.27) | copy-start | bytes 12582916
  436.6 1.1 copy-start.11
  436.6 1.9 copy-start.17
  436.6 2.7 copy-start.19
  436.6 3.5 copy-start.21
  453.5 62.2 %copy-start.25 = (f32[2048]{0:T(1024)S(1)}, f32[2048]{0:T(1024)}, u32[]{:S(2)}) copy-start(f32[2048]{0:T(1024)} %param.28) | copy-start | bytes 24580
  453.5 65.2 %copy-start.1 = (bf16[2048,768]{1,0:T(8,128)(2,1)S(1)}, bf16[2048,768]{1,0:T(8,128)(2,1)}, u32[]{:S(2)}) copy-start(bf16[2048,768]{1,0:T(8,128)(2,1)} %param.19) | copy-start | bytes 9437188
Sparse Core Ops, SparseCore 0:
  13.3 84.7 all-gather.3
  144.8 88.1 reduce-scatter.6
  235.3 82.8 reduce-scatter.4
  320.3 46.0 all-gather.5
  368.4 45.7 all-gather.7
  416.3 48.8 reduce-scatter.8
  467.5 48.1 reduce-scatter.10
